TPU v7x, 256 devices: a whole 4x4x8 slice. The times are simulated.
256 devices in a mesh: tp: 16 (over x_lo, y, core), grp: 16 (over z, x_hi).
Axes of the slice: x: 4 (x_hi: 2, x_lo: 2; x = x_hi * 2 + x_lo), y: 4, z: 8, core: 2. Of those that a mesh axis runs over, the one named last changes fastest.
Arguments:
- resid_in: bfloat16 [1024, 8192], P('grp', 'tp'), may hold values from -6 to 6
- queries: bfloat16 [1024, 4096], P('grp', 'tp')
- kv_cache: bfloat16 [2, 1024, 16, 128, 128], P(None, 'grp', 'tp'), as said below
- new_kv: bfloat16 [2, 1024, 4, 128], P(None, 'grp')
- lengths: int32 [1024], P('grp'), may hold values from 1 to 128, 65536 in all
- out_weight: bfloat16 [4096, 8192], P('tp'), may hold values from -0.09375 to 0.09375
- enc_weight: bfloat16 [8192, 32768], P('tp', 'grp'), may hold values from -0.0625 to 0.0625
- enc_bias: float32 [32768], P('grp'), may hold values from -1 to 0.5
- dec_weight: bfloat16 [32768, 8192], P('grp', 'tp'), may hold values from -0.75 to 0.75
- clamp_ids: int32 [1024, 4], P('grp'), may hold values from 0 to 32767, as said below
- clamp_values: float32 [1024, 4], P('grp'), may hold values from 2 to 8
Outputs:
- resid_out: bfloat16 [1024, 8192], P('grp', 'tp')
- features: bfloat16 [1024, 32768], P('tp', 'grp')
Inputs may be any that keep to these rules, and one draw needn't show every extreme that they name: Entries of kv_cache whose third index divided by 4 agrees are equal. `clamp_ids`: a row's 4 ids are (b + c * 8192) modulo 32768 for c = 0 .. 3.
All inputs are finite; a program needn't handle non-finite values. No bound on the sum of `lengths` on one device may be relied on, other than what follows from the above.
Results may differ from a plain program's by a relative error of at most 0.008.
Values may be sent and summed in bfloat16 or wider, within the bound.
No kernel may reach another device: no remote copies, remote signals or barrier semaphores. Data moves between devices by JAX's collectives and lax.ppermute only.
A program may use at most 128 MiB of HBM per device.

v0:
```python
import jax
import jax.numpy as jnp
from jax import lax
from jax.sharding import PartitionSpec as P

HEAD_DIM = 128
KV_HEADS = 4


def clamp_delta(latent_block, id_table, value_table, offset):
    width = latent_block.shape[1]
    columns = jnp.arange(width, dtype=jnp.int32)
    local_ids = id_table - offset
    current = latent_block.astype(jnp.float32)
    delta_total = jnp.zeros(latent_block.shape, jnp.float32)
    for slot_index in range(id_table.shape[1]):
        is_hit = columns[None, :] == local_ids[:, slot_index : slot_index + 1]
        clamped_now = jnp.sum(jnp.where(is_hit, current, 0.0), axis=1, keepdims=True)
        delta_total = delta_total + jnp.where(
            is_hit, value_table[:, slot_index : slot_index + 1] - clamped_now, 0.0
        )
    return delta_total.astype(jnp.bfloat16)


def per_device(
    resid_in,
    queries,
    kv_cache,
    new_kv,
    lengths,
    out_weight,
    enc_weight,
    enc_bias,
    dec_weight,
    clamp_ids,
    clamp_values,
):
    tp_count = lax.axis_size("tp")
    tp_rank = lax.axis_index("tp")
    grp_rank = lax.axis_index("grp")
    row_count = resid_in.shape[0]
    own_heads = queries.shape[1] // HEAD_DIM
    slot_count = kv_cache.shape[3]
    score_scale = HEAD_DIM ** (-0.5)
    query_heads = queries.reshape(row_count, own_heads, HEAD_DIM)
    cache_keys = kv_cache[0, :, 0]
    cache_values = kv_cache[1, :, 0]
    kv_index = tp_rank // (tp_count // KV_HEADS)
    new_key = lax.dynamic_index_in_dim(new_kv[0], kv_index, 1, keepdims=False)
    new_value = lax.dynamic_index_in_dim(new_kv[1], kv_index, 1, keepdims=False)
    scores = (
        jnp.einsum("shd,spd->shp", query_heads, cache_keys, preferred_element_type=jnp.float32)
        * score_scale
    )
    new_score = (
        jnp.einsum("shd,sd->sh", query_heads, new_key, preferred_element_type=jnp.float32)
        * score_scale
    )
    slot_index = jnp.arange(slot_count, dtype=jnp.int32)
    is_valid = (slot_index[None, :] < lengths[:, None])[:, None, :]
    top_score = jnp.maximum(jnp.max(jnp.where(is_valid, scores, -jnp.inf), axis=-1), new_score)
    prob_cache = jnp.where(is_valid, jnp.exp(scores - top_score[..., None]), 0.0)
    new_prob = jnp.exp(new_score - top_score)
    total_weight = jnp.sum(prob_cache, axis=-1) + new_prob
    new_rounded = lax.optimization_barrier(new_prob.astype(jnp.bfloat16)).astype(jnp.float32)
    weighted = jnp.einsum(
        "shp,spd->shd",
        prob_cache.astype(jnp.bfloat16),
        cache_values,
        preferred_element_type=jnp.float32,
    )
    weighted = weighted + new_rounded[..., None] * new_value.astype(jnp.float32)[:, None, :]
    head_output = (
        (weighted / total_weight[..., None])
        .astype(jnp.bfloat16)
        .reshape(row_count, own_heads * HEAD_DIM)
    )
    attn_part = jnp.dot(head_output, out_weight, preferred_element_type=jnp.float32)
    attn_cols = lax.psum_scatter(attn_part, "tp", scatter_dimension=1, tiled=True)
    resid_mid = (resid_in.astype(jnp.float32) + attn_cols).astype(jnp.bfloat16)
    id_table, value_table = (
        lax.all_gather(clamp_ids, "grp", axis=0, tiled=True),
        lax.all_gather(clamp_values, "grp", axis=0, tiled=True),
    )
    pre_part = jnp.dot(
        lax.all_gather(resid_mid, "grp", axis=0, tiled=True),
        enc_weight,
        preferred_element_type=jnp.float32,
    )
    all_rows = pre_part.shape[0]
    lat_span = enc_weight.shape[1]
    span_start = grp_rank * lat_span
    pre_act = lax.psum(pre_part, "tp")
    latent_block = jnp.maximum(pre_act + enc_bias, 0.0).astype(jnp.bfloat16)
    out_rows = all_rows // tp_count
    feature_out = lax.dynamic_slice_in_dim(latent_block, tp_rank * out_rows, out_rows, 0)
    delta_lat = clamp_delta(latent_block, id_table, value_table, span_start)
    edit_part = jnp.dot(delta_lat, dec_weight, preferred_element_type=jnp.float32)
    edit_whole = lax.psum(edit_part, "grp")
    edit_mine = lax.dynamic_slice_in_dim(edit_whole, grp_rank * row_count, row_count, 0)
    resid_out = (resid_mid.astype(jnp.float32) + edit_mine).astype(jnp.bfloat16)
    return (resid_out, feature_out)


def solution(mesh):
    placed = (
        P("grp", "tp"),
        P("grp", "tp"),
        P(None, "grp", "tp", None, None),
        P(None, "grp", None, None),
        P("grp"),
        P("tp", None),
        P("tp", "grp"),
        P("grp"),
        P("grp", "tp"),
        P("grp", None),
        P("grp", None),
    )
    return jax.shard_map(
        per_device,
        mesh=mesh,
        in_specs=placed,
        out_specs=(P("grp", "tp"), P("tp", "grp")),
        check_vma=False,
    )
```

profile of v0, /device:TPU:8, one launch (start us, length us, event | category | flops | bytes accessed | tf_op | source)
XLA Modules:
  0.0 511.2 jit_solution(2312959779147829518)
XLA Ops:
  7.2 0.0 copy-start
  7.2 0.0 reduce-scatter.2.cloned.1.call-start
  7.3 1.1 fusion.30
  8.3 0.1 dynamic-slice_convert_fusion
  8.4 0.8 reshape.42
  9.2 0.9 iota_compare_fusion.4
  10.1 0.2 fusion.24
  10.3 3.0 select_reduce_fusion
  13.3 0.2 fusion.29
  13.6 2.3 fusion.19
  15.9 2.2 fusion.20
  18.1 0.0 reduce-scatter.2.cloned.1.call-update
  18.1 0.0 all-gather.4.cloned.1.call-start
  18.2 65.8 %reduce-scatter.2.cloned.1.call-done = f32[64,512]{1,0:T(8,128)} async-done(((f32[64,8192]{1,0:T(8,128)}), f32[64,512]{1,0:T(8,128)}) %reduce-scatter.2.cloned.1.call-update) | async-done | bytes 131088 | tf_op jit(solution)/shard_map/reduce_scatter | solution.py:79
  84.0 1.5 add_convert_fusion.3
  85.6 0.0 all-gather.4.cloned.1.call-update
  85.6 0.0 all-reduce.3.cloned.1.call-start
  85.7 82.6 %all-gather.4.cloned.1.call-done = bf16[1024,512]{1,0:T(8,128)(2,1)} async-done(((bf16[64,512]{1,0:T(8,128)(2,1)}), bf16[1024,512]{1,0:T(8,128)(2,1)}) %all-gather.4.cloned.1.call-update) | async-done | bytes 1048592 | tf_op jit(solution)/shard_map/all_gather | solution.py:86
  168.2 6.8 %fusion.32 = f32[1024,2048]{1,0:T(8,128)} fusion(bf16[1024,512]{1,0:T(8,128)(2,1)} %all-gather.4.cloned.1.call-done, bf16[512,2048]{1,0:T(8,128)(2,1)S(1)} %copy-done), kind=kOutput, calls=%fused_computation.60 | convolution fusion | flops 2147483648 | bytes 11534336 | tf_op jit(solution)/shard_map/dot_general | solution.py:85
  175.0 0.0 all-reduce.3.cloned.1.call-update
  175.0 0.0 all-reduce.5.cloned.1.call-start
  175.1 37.5 %all-gather = s32[16,64,4]{1,2,0:T(4,128)S(1)} all-gather(s32[1,64,4]{1,2,0:T(4,128)S(1)} %bitcast.75), channel_id=1, replica_groups=mesh['tp'=16,'grp'=16] {'grp'}, dimensions={0}, use_global_device_ids=true | all-gather | bytes 17408 | tf_op jit(solution)/shard_map/all_gather | solution.py:82
  212.6 0.1 reshape.50
  212.7 37.4 %all-gather.1 = f32[16,64,4]{1,2,0:T(4,128)S(1)} all-gather(f32[1,64,4]{1,2,0:T(4,128)S(1)} %bitcast.76), channel_id=1, replica_groups=mesh['tp'=16,'grp'=16] {'grp'}, dimensions={0}, use_global_device_ids=true | all-gather | bytes 17408 | tf_op jit(solution)/shard_map/all_gather | solution.py:83
  250.1 0.1 reshape.48
  250.2 66.4 %all-reduce.3.cloned.1.call-done = f32[1024,2048]{1,0:T(8,128)} async-done(((f32[1024,2048]{1,0:T(8,128)}), f32[1024,2048]{1,0:T(8,128)}) %all-reduce.3.cloned.1.call-update) | async-done | bytes 8388624 | tf_op jit(solution)/shard_map/psum | solution.py:93
  316.6 9.0 %fusion = (f32[1024]{0:T(1024)S(1)}, f32[1024]{0:T(1024)S(1)}, f32[1024]{0:T(1024)S(1)}, f32[1024]{0:T(1024)S(1)}, bf16[1024,2048]{1,0:T(8,128)(2,1)}) fusion(s32[1024]{0:T(1024)S(1)} %bitcast.68, s32[1024]{0:T(1024)S(1)} %bitcast.66, s32[1024]{0:T(1024)S(1)} %bitcast.64, s32[1024]{0:T(1024)S(1)} %bitcast.62, f32[1024,2048]{1,0:T(8,128)} %all-reduce.3.cloned.1.call-done, ...), kind=kLoop, calls=%fused_computation.4 | loop fusion | flops 33550336 | bytes 12623872 | tf_op jit(solution)/shard_map/reduce_sum | solution.py:18
  325.6 6.1 %fusion.4 = f32[1024,512]{1,0:T(8,128)} fusion(bf16[2048,512]{1,0:T(8,128)(2,1)S(1)} %copy-done.7, f32[1024]{0:T(1024)S(1)} %bitcast.72, s32[1024]{0:T(1024)S(1)} %bitcast.63, f32[1024]{0:T(1024)S(1)} %bitcast.73, s32[1024]{0:T(1024)S(1)} %bitcast.65, f32[1024]{0:T(1024)S(1)} %bitcast.74, s32[1024]{0:T(1024)S(1)} %bitcast.67, f32[1024]{0:T(1024)S(1)} %bitcast.71, ...), kind=kOutput, calls=%fused_computation.14 | convolution fusion | flops 2172649472 | bytes 4227072 | tf_op jit(solution)/shard_map/dot_general | solution.py:98
  331.7 0.0 all-reduce.5.cloned.1.call-update
  331.7 1.7 constant_dynamic-slice_fusion
  333.4 169.7 %all-reduce.5.cloned.1.call-done = f32[1024,512]{1,0:T(8,128)} async-done(((f32[1024,512]{1,0:T(8,128)}), f32[1024,512]{1,0:T(8,128)}) %all-reduce.5.cloned.1.call-update) | async-done | bytes 2097168 | tf_op jit(solution)/shard_map/psum | solution.py:99
  503.1 1.5 add_convert_fusion.2
  (23 shorter events, 0.1 us)
Async XLA Ops:
  7.2 161.1 %copy-start = (bf16[512,2048]{1,0:T(8,128)(2,1)S(1)}, bf16[512,2048]{1,0:T(8,128)(2,1)}, u32[]{:S(2)}) copy-start(bf16[512,2048]{1,0:T(8,128)(2,1)} %param.17) | copy-start | bytes 6291460
  7.2 76.8 %copy-start.3 = (bf16[64,512]{1,0:T(8,128)(2,1)S(1)}, bf16[64,512]{1,0:T(8,128)(2,1)}, u32[]{:S(2)}) copy-start(bf16[64,512]{1,0:T(8,128)(2,1)} %param.11) | copy-start | bytes 196612
  7.2 76.8 %reduce-scatter.2.cloned.1.call-start = ((), (), s32[]{:S(2)}) async-start(), calls=%async_computation.1 | async-start | bytes 2228224 | tf_op jit(solution)/shard_map/reduce_scatter | solution.py:79
  9.2 6.7 %copy-start.1 = (bf16[256,8192]{1,0:T(8,128)(2,1)S(1)}, bf16[256,8192]{1,0:T(8,128)(2,1)}, u32[]{:S(2)}) copy-start(bf16[256,8192]{1,0:T(8,128)(2,1)} %param.16) | copy-start | bytes 12582916
  18.1 150.1 %all-gather.4.cloned.1.call-start = ((), (), s32[]{:S(2)}) async-start(), calls=%async_computation.2 | async-start | bytes 1114112 | tf_op jit(solution)/shard_map/all_gather | solution.py:86
  85.6 89.5 %copy-start.5 = (s32[64,4]{0,1:T(4,128)S(1)}, s32[64,4]{0,1:T(4,128)}, u32[]{:S(2)}) copy-start(s32[64,4]{0,1:T(4,128)} %param.20) | copy-start | bytes 3076
  85.6 127.1 %copy-start.6 = (f32[64,4]{0,1:T(4,128)S(1)}, f32[64,4]{0,1:T(4,128)}, u32[]{:S(2)}) copy-start(f32[64,4]{0,1:T(4,128)} %param.21) | copy-start | bytes 3076
  85.6 231.0 %copy-start.4 = (f32[2048]{0:T(1024)S(1)}, f32[2048]{0:T(1024)}, u32[]{:S(2)}) copy-start(f32[2048]{0:T(1024)} %param.18) | copy-start | bytes 24580
  85.6 231.0 %all-reduce.3.cloned.1.call-start = ((), (), s32[]{:S(2)}) async-start(), calls=%async_computation.3 | async-start | bytes 16777216 | tf_op jit(solution)/shard_map/psum | solution.py:93
  175.0 328.0 %all-reduce.5.cloned.1.call-start = ((), (), s32[]{:S(2)}) async-start(), calls=%async_computation.4 | async-start | bytes 4194304 | tf_op jit(solution)/shard_map/psum | solution.py:99
  316.6 9.0 %copy-start.7 = (bf16[2048,512]{1,0:T(8,128)(2,1)S(1)}, bf16[2048,512]{1,0:T(8,128)(2,1)}, u32[]{:S(2)}) copy-start(bf16[2048,512]{1,0:T(8,128)(2,1)} %param.19) | copy-start | bytes 6291460
  325.6 177.5 %copy-start.2 = (bf16[64,512]{1,0:T(8,128)(2,1)S(1)}, bf16[64,512]{1,0:T(8,128)(2,1)}, u32[]{:S(2)}) copy-start(bf16[64,512]{1,0:T(8,128)(2,1)} %add_convert_fusion.3) | copy-start | bytes 196612
Sparse Core Ops, SparseCore 0:
  18.3 65.6 reduce-scatter.1
  87.2 81.0 all-gather.3
  175.2 141.4 all-reduce.2
  331.9 171.1 all-reduce.4
where the time goes:
time: 512 us; the launch traced here: 511 us
  waiting for transfers between devices  385 us (75%)
  blocking collectives  74.9 us (15%)
  matrix products  20.6 us (4%)
  between operations  13.9 us (3%)
  other arithmetic  13.3 us (3%)
    psum x1, waiting for transfers between devices, per_device(): edit_whole = lax.psum(edit_part, 'grp')  170 us
    all_gather x1, waiting for transfers between devices, per_device(): lax.all_gather(resid_mid, 'grp', axis=0, tiled=True)  82.6 us
    psum x1, waiting for transfers between devices, per_device(): pre_act = lax.psum(pre_part, 'tp')  66.4 us
    reduce_scatter x1, waiting for transfers between devices, per_device(): lax.psum_scatter(attn_part, 'tp', scatter_dimension=1, tiled=True)  65.8 us
    all_gather x1, blocking collectives, per_device(): lax.all_gather(clamp_ids, 'grp', axis=0, tiled=True)  37.5 us
    all_gather x1, blocking collectives, per_device(): lax.all_gather(clamp_values, 'grp', axis=0, tiled=True)  37.4 us
  transfers between devices with their start and end apart: 4, of which 4 were waited for; matrix products, arithmetic and copies ran while one was open for 0% of the time, Pallas kernels for 0%

commit v1 on v0

--- a/solution.py
+++ b/solution.py
@@ -80,7 +80,9 @@
     resid_mid = (resid_in.astype(jnp.float32) + attn_cols).astype(jnp.bfloat16)
     id_table, value_table = (
         lax.all_gather(clamp_ids, "grp", axis=0, tiled=True),
-        lax.all_gather(clamp_values, "grp", axis=0, tiled=True),
+        jnp.concatenate(
+            lax.all_to_all(jnp.stack([clamp_values] * lax.axis_size("grp")), "grp", 0, 0), axis=0
+        ),
     )
     pre_part = jnp.dot(
         lax.all_gather(resid_mid, "grp", axis=0, tiled=True),

time: 512 us -> 511 us (level)
  blocking collectives: 74.9 us -> 41.2 us
  waiting for transfers between devices: 385 us -> 412 us
    all_gather x1 -> x0, blocking collectives: 37.4 us -> none  [per_device(): lax.all_gather(clamp_values, 'grp', axis=0, tiled=True)]
    psum x1, waiting for transfers between devices: 66.4 us -> 93.4 us  [per_device(): pre_act = lax.psum(pre_part, 'tp')]
  transfers between devices with their start and end apart: 4 -> 5, of which waited for: 4 -> 4; matrix products, arithmetic and copies ran while one was open for 0% -> 1% of each run, Pallas kernels for 0% -> 0%
where the time goes in v1:
time: 511 us
  waiting for transfers between devices  412 us (81%)
  blocking collectives  41.2 us (8%)
  matrix products  20.6 us (4%)
  other arithmetic  14 us (3%)
  between operations  14 us (3%)
    psum x1, waiting for transfers between devices, per_device(): edit_whole = lax.psum(edit_part, 'grp')  170 us
    psum x1, waiting for transfers between devices, per_device(): pre_act = lax.psum(pre_part, 'tp')  93.4 us
    all_gather x1, waiting for transfers between devices, per_device(): lax.all_gather(resid_mid, 'grp', axis=0, tiled=True)  82.6 us
    reduce_scatter x1, waiting for transfers between devices, per_device(): lax.psum_scatter(attn_part, 'tp', scatter_dimension=1, tiled=True)  65.8 us
    all_gather x1, blocking collectives, per_device(): lax.all_gather(clamp_ids, 'grp', axis=0, tiled=True)  41.2 us
  transfers between devices with their start and end apart: 5, of which 4 were waited for; matrix products, arithmetic and copies ran while one was open for 1% of the time, Pallas kernels for 0%

profile of v1, /device:TPU:8, one launch (start us, length us, event | category | flops | bytes accessed | tf_op | source)
XLA Modules:
  0.0 510.6 jit_solution(12093215585327898740)
XLA Ops:
  7.2 0.0 reduce-scatter.2.cloned.1.call-start
  7.3 1.1 fusion.30
  8.3 0.1 dynamic-slice_convert_fusion
  8.4 0.8 reshape.47
  9.2 0.9 iota_compare_fusion.4
  10.1 0.2 fusion.24
  10.3 3.0 select_reduce_fusion
  13.3 0.2 fusion.29
  13.6 2.3 fusion.19
  15.9 2.2 fusion.20
  18.1 0.0 reduce-scatter.2.cloned.1.call-update
  18.2 0.0 all-gather.3.cloned.1.call-start
  18.2 65.8 %reduce-scatter.2.cloned.1.call-done = f32[64,512]{1,0:T(8,128)} async-done(((f32[64,8192]{1,0:T(8,128)}), f32[64,512]{1,0:T(8,128)}) %reduce-scatter.2.cloned.1.call-update) | async-done | bytes 131088 | tf_op jit(solution)/shard_map/reduce_scatter | solution.py:79
  84.0 1.5 add_convert_fusion.3
  85.6 0.0 all-reduce.3.cloned.1.call-start
  85.6 82.6 %all-gather.3.cloned.1.call-done = bf16[1024,512]{1,0:T(8,128)(2,1)} async-done(((bf16[64,512]{1,0:T(8,128)(2,1)}), bf16[1024,512]{1,0:T(8,128)(2,1)}) %all-gather.3.cloned.1.call-update) | async-done | bytes 1048592 | tf_op jit(solution)/shard_map/all_gather | solution.py:88
  168.2 6.8 %fusion.32 = f32[1024,2048]{1,0:T(8,128)} fusion(bf16[1024,512]{1,0:T(8,128)(2,1)} %all-gather.3.cloned.1.call-done, bf16[512,2048]{1,0:T(8,128)(2,1)S(1)} %copy-done), kind=kOutput, calls=%fused_computation.61 | convolution fusion | flops 2147483648 | bytes 11534336 | tf_op jit(solution)/shard_map/dot_general | solution.py:87
  175.1 0.7 reshape.57
  175.8 4.1 all-to-all-start
  179.9 0.0 all-reduce.5.cloned.1.call-start
  180.0 41.2 %all-gather = s32[16,64,4]{1,2,0:T(4,128)S(1)} all-gather(s32[1,64,4]{1,2,0:T(4,128)S(1)} %bitcast.78), channel_id=1, replica_groups=mesh['tp'=16,'grp'=16] {'grp'}, dimensions={0}, use_global_device_ids=true | all-gather | bytes 17408 | tf_op jit(solution)/shard_map/all_gather | solution.py:82
  221.2 0.1 reshape.54
  221.3 0.5 broadcast.19
  221.8 0.7 reduce
  222.5 0.1 reshape.58
  222.6 0.1 reshape.49
  222.7 93.4 %all-reduce.3.cloned.1.call-done = f32[1024,2048]{1,0:T(8,128)} async-done(((f32[1024,2048]{1,0:T(8,128)}), f32[1024,2048]{1,0:T(8,128)}) %all-reduce.3.cloned.1.call-update) | async-done | bytes 8388624 | tf_op jit(solution)/shard_map/psum | solution.py:95
  316.1 9.0 %fusion = (f32[1024]{0:T(1024)S(1)}, f32[1024]{0:T(1024)S(1)}, f32[1024]{0:T(1024)S(1)}, f32[1024]{0:T(1024)S(1)}, bf16[1024,2048]{1,0:T(8,128)(2,1)}) fusion(s32[1024]{0:T(1024)S(1)} %bitcast.71, s32[1024]{0:T(1024)S(1)} %bitcast.69, s32[1024]{0:T(1024)S(1)} %bitcast.67, s32[1024]{0:T(1024)S(1)} %bitcast.65, f32[1024,2048]{1,0:T(8,128)} %all-reduce.3.cloned.1.call-done, ...), kind=kLoop, calls=%fused_computation.4 | loop fusion | flops 33550336 | bytes 12623872 | tf_op jit(solution)/shard_map/reduce_sum | solution.py:18
  325.1 6.1 %fusion.4 = f32[1024,512]{1,0:T(8,128)} fusion(bf16[2048,512]{1,0:T(8,128)(2,1)S(1)} %copy-done.7, f32[1024]{0:T(1024)S(1)} %bitcast.75, s32[1024]{0:T(1024)S(1)} %bitcast.66, f32[1024]{0:T(1024)S(1)} %bitcast.76, s32[1024]{0:T(1024)S(1)} %bitcast.68, f32[1024]{0:T(1024)S(1)} %bitcast.77, s32[1024]{0:T(1024)S(1)} %bitcast.70, f32[1024]{0:T(1024)S(1)} %bitcast.74, ...), kind=kOutput, calls=%fused_computation.14 | convolution fusion | flops 2172649472 | bytes 4227072 | tf_op jit(solution)/shard_map/dot_general | solution.py:100
  331.2 1.7 constant_dynamic-slice_fusion
  332.9 169.7 %all-reduce.5.cloned.1.call-done = f32[1024,512]{1,0:T(8,128)} async-done(((f32[1024,512]{1,0:T(8,128)}), f32[1024,512]{1,0:T(8,128)}) %all-reduce.5.cloned.1.call-update) | async-done | bytes 2097168 | tf_op jit(solution)/shard_map/psum | solution.py:101
  502.6 1.5 add_convert_fusion.2
  (29 shorter events, 0.2 us)
Async XLA Ops:
  7.2 161.1 %copy-start = (bf16[512,2048]{1,0:T(8,128)(2,1)S(1)}, bf16[512,2048]{1,0:T(8,128)(2,1)}, u32[]{:S(2)}) copy-start(bf16[512,2048]{1,0:T(8,128)(2,1)} %param.17) | copy-start | bytes 6291460
  7.2 76.8 %copy-start.3 = (bf16[64,512]{1,0:T(8,128)(2,1)S(1)}, bf16[64,512]{1,0:T(8,128)(2,1)}, u32[]{:S(2)}) copy-start(bf16[64,512]{1,0:T(8,128)(2,1)} %param.11) | copy-start | bytes 196612
  7.2 76.8 %reduce-scatter.2.cloned.1.call-start = ((), (), s32[]{:S(2)}) async-start(), calls=%async_computation.2 | async-start | bytes 2228224 | tf_op jit(solution)/shard_map/reduce_scatter | solution.py:79
  9.2 6.7 %copy-start.1 = (bf16[256,8192]{1,0:T(8,128)(2,1)S(1)}, bf16[256,8192]{1,0:T(8,128)(2,1)}, u32[]{:S(2)}) copy-start(bf16[256,8192]{1,0:T(8,128)(2,1)} %param.16) | copy-start | bytes 12582916
  18.2 150.1 %all-gather.3.cloned.1.call-start = ((), (), s32[]{:S(2)}) async-start(), calls=%async_computation.3 | async-start | bytes 1114112 | tf_op jit(solution)/shard_map/all_gather | solution.py:88
  85.6 89.5 %copy-start.5 = (f32[64,4]{0,1:T(4,128)S(1)}, f32[64,4]{0,1:T(4,128)}, u32[]{:S(2)}) copy-start(f32[64,4]{0,1:T(4,128)} %param.21) | copy-start | bytes 3076
  85.6 94.4 %copy-start.6 = (s32[64,4]{0,1:T(4,128)S(1)}, s32[64,4]{0,1:T(4,128)}, u32[]{:S(2)}) copy-start(s32[64,4]{0,1:T(4,128)} %param.20) | copy-start | bytes 3076
  85.6 230.5 %copy-start.4 = (f32[2048]{0:T(1024)S(1)}, f32[2048]{0:T(1024)}, u32[]{:S(2)}) copy-start(f32[2048]{0:T(1024)} %param.18) | copy-start | bytes 24580
  85.6 230.5 %all-reduce.3.cloned.1.call-start = ((), (), s32[]{:S(2)}) async-start(), calls=%async_computation.4 | async-start | bytes 16777216 | tf_op jit(solution)/shard_map/psum | solution.py:95
  175.8 45.5 %all-to-all-start = ((f32[16,1,256]{2,1,0:T(1,128)}), f32[16,1,256]{2,1,0:T(1,128)S(1)}, u32[]{:S(2)}, u32[]{:S(2)}) async-start(f32[16,1,256]{2,1,0:T(1,128)} %reshape.57), calls=%async_computation.1 | async-start | bytes 32768 | tf_op jit(solution)/shard_map/all_to_all | solution.py:84
  179.9 322.7 %all-reduce.5.cloned.1.call-start = ((), (), s32[]{:S(2)}) async-start(), calls=%async_computation.5 | async-start | bytes 4194304 | tf_op jit(solution)/shard_map/psum | solution.py:101
  316.1 9.0 %copy-start.7 = (bf16[2048,512]{1,0:T(8,128)(2,1)S(1)}, bf16[2048,512]{1,0:T(8,128)(2,1)}, u32[]{:S(2)}) copy-start(bf16[2048,512]{1,0:T(8,128)(2,1)} %param.19) | copy-start | bytes 6291460
  325.1 177.5 %copy-start.2 = (bf16[64,512]{1,0:T(8,128)(2,1)S(1)}, bf16[64,512]{1,0:T(8,128)(2,1)}, u32[]{:S(2)}) copy-start(bf16[64,512]{1,0:T(8,128)(2,1)} %add_convert_fusion.3) | copy-start | bytes 196612
Sparse Core Ops, SparseCore 0:
  18.3 65.6 reduce-scatter.1
  87.1 81.0 all-gather.2
  175.2 140.8 all-reduce.2
  331.3 171.2 all-reduce.4
